TPU v7x, 512 devices: a whole 4x4x16 slice. The times are simulated.
512 devices in a mesh: node: 16 (over z), cuts: 32 (over x, y, core).
Axes of the slice: x: 4, y: 4, z: 16, core: 2. Of those that a mesh axis runs over, the one named last changes fastest.
Arguments:
- core_x: bfloat16 [32, 256, 256, 256], P('node', 'cuts'), may hold values from -6 to 6
- core_y: bfloat16 [32, 256, 256, 256], P('node', 'cuts'), may hold values from -0.0234375 to 0.0234375
- left_intersection: bfloat16 [32, 256, 256], P('node', 'cuts'), may hold values from -0.375 to 0.375
- right_intersection: bfloat16 [32, 256, 256], P('node', 'cuts'), may hold values from -0.375 to 0.375
Outputs:
- parent_intersection: float32 [32, 256, 256], P('node', 'cuts')
All inputs are finite; a program needn't handle non-finite values.
Results may differ from a plain program's by a relative error of at most 0.004.
Values may be sent and summed in bfloat16 or wider, within the bound.
A program may use at most 64 MiB of HBM per device.

v0:
```python
import jax
import jax.numpy as jnp
from jax import lax
from jax.sharding import PartitionSpec as P


def shards(core_x, core_y, left_intersection, right_intersection):
    left_full = lax.all_gather(left_intersection, "cuts", axis=1, tiled=True)
    first = jnp.einsum(
        "pik,paij->pakj", left_full, core_x, preferred_element_type=jnp.float32
    ).astype(jnp.bfloat16)
    right_full = lax.all_gather(right_intersection, "cuts", axis=1, tiled=True)
    moved = lax.all_to_all(
        jnp.einsum("pakj,pjl->pakl", first, right_full, preferred_element_type=jnp.float32).astype(
            jnp.bfloat16
        ),
        "cuts",
        split_axis=2,
        concat_axis=1,
        tiled=True,
    )
    mine = lax.psum_scatter(
        jnp.einsum("pakl,pklb->apb", moved, core_y, preferred_element_type=jnp.float32),
        "cuts",
        scatter_dimension=0,
        tiled=True,
    )
    return jnp.transpose(mine, (1, 0, 2))


def solution(mesh):
    return jax.shard_map(
        shards,
        mesh=mesh,
        in_specs=(
            P("node", "cuts", None, None),
            P("node", "cuts", None, None),
            P("node", "cuts", None),
            P("node", "cuts", None),
        ),
        out_specs=P("node", "cuts", None),
        check_vma=False,
    )
```

profile of v0, /device:TPU:1, one launch (start us, length us, event | category | flops | bytes accessed | tf_op | source)
XLA Modules:
  0.0 202.5 jit_solution(18417763464070632930)
XLA Ops:
  6.5 0.0 copy-start
  6.5 0.0 reduce-scatter.2.cloned.1.call-start
  6.5 27.7 %all_gather.6 = bf16[2,256,256]{2,1,0:T(8,128)(2,1)S(1)} all-gather(bf16[2,8,256]{2,1,0:T(8,128)(2,1)} %param.6), channel_id=1, replica_groups=mesh['node'=16,'cuts'=32] {'cuts'}, dimensions={1}, use_global_device_ids=true | all-gather | bytes 270336 | tf_op jit(solution)/shard_map/all_gather | solution.py:8
  34.2 25.6 %all_gather.7 = bf16[2,256,256]{2,1,0:T(8,128)(2,1)S(1)} all-gather(bf16[2,8,256]{2,1,0:T(8,128)(2,1)} %param.7), channel_id=1, replica_groups=mesh['node'=16,'cuts'=32] {'cuts'}, dimensions={1}, use_global_device_ids=true | all-gather | bytes 270336 | tf_op jit(solution)/shard_map/all_gather | solution.py:12
  59.8 0.0 copy-done
  59.8 2.6 %fusion.8 = bf16[2,8,256,256]{3,2,1,0:T(8,128)(2,1)} fusion(bf16[2,8,256,256]{3,2,1,0:T(8,128)(2,1)S(1)} %copy-done, bf16[2,256,256]{2,1,0:T(8,128)(2,1)S(1)} %all_gather.7, bf16[2,256,256]{2,1,0:T(8,128)(2,1)S(1)} %all_gather.6), kind=kOutput, calls=%fused_computation.7 | convolution fusion | flops 1075838976 | bytes 4718592 | tf_op jit(solution)/shard_map/pakj,pjl->pakl/dot_general | solution.py:14
  62.4 2.8 %copy.6 = bf16[2,8,256,256]{3,1,0,2:T(8,128)(2,1)S(1)} copy(bf16[2,8,256,256]{3,2,1,0:T(8,128)(2,1)} %fusion.8) | data formatting | bytes 4194304 | tf_op jit(solution)/shard_map/convert_element_type | solution.py:14
  65.2 0.0 copy-start.1
  65.2 32.3 %all_to_all.18 = bf16[2,8,256,256]{3,1,0,2:T(8,128)(2,1)S(1)} all-to-all(bf16[2,8,256,256]{3,1,0,2:T(8,128)(2,1)S(1)} %copy.6), channel_id=1, replica_groups=mesh['node'=16,'cuts'=32] {'cuts'}, dimensions={2} | all-to-all | bytes 4194304 | tf_op jit(solution)/shard_map/all_to_all | solution.py:13
  97.5 0.0 copy-done.1
  97.5 1.5 fusion.11
  99.0 0.0 reduce-scatter.2.cloned.1.call-update
  99.1 96.6 %reduce-scatter.2.cloned.1.call-done = f32[8,2,256]{2,0,1:T(8,128)} async-done(((f32[256,2,256]{2,0,1:T(8,128)}), f32[8,2,256]{2,0,1:T(8,128)}) %reduce-scatter.2.cloned.1.call-update) | async-done | bytes 16400 | tf_op jit(solution)/shard_map/reduce_scatter | solution.py:22
Async XLA Ops:
  6.5 53.3 %copy-start = (bf16[2,8,256,256]{3,2,1,0:T(8,128)(2,1)S(1)}, bf16[2,8,256,256]{3,2,1,0:T(8,128)(2,1)}, u32[]{:S(2)}) copy-start(bf16[2,8,256,256]{3,2,1,0:T(8,128)(2,1)} %param.4) | copy-start | bytes 6291460
  6.5 189.2 %reduce-scatter.2.cloned.1.call-start = ((), (), s32[]{:S(2)}) async-start(), calls=%async_computation.2 | async-start | bytes 540672 | tf_op jit(solution)/shard_map/reduce_scatter | solution.py:22
  65.2 32.3 %copy-start.1 = (bf16[2,8,256,256]{3,2,1,0:T(8,128)(2,1)S(1)}, bf16[2,8,256,256]{3,2,1,0:T(8,128)(2,1)}, u32[]{:S(2)}) copy-start(bf16[2,8,256,256]{3,2,1,0:T(8,128)(2,1)} %param.5) | copy-start | bytes 6291460
Sparse Core Ops, SparseCore 0:
  99.2 96.4 reduce-scatter.1
where the time goes:
time: 204 us; the launch traced here: 203 us
  waiting for transfers between devices  96.6 us (47%)
  blocking collectives  85.6 us (42%)
  between operations  13.4 us (7%)
  matrix products  4.16 us (2%)
  local copies, waits for them, and re-layouts  2.78 us (1%)
    reduce_scatter x1, waiting for transfers between devices, shards(): lax.psum_scatter(jnp.einsum('pakl,pklb->apb', moved, core_y, preferred_el...  96.6 us
    all_to_all x1, blocking collectives, shards(): lax.all_to_all(jnp.einsum('pakj,pjl->pakl', first, right_full, preferred_...  32.3 us
    all_gather x1, blocking collectives, shards(): left_full = lax.all_gather(left_intersection, 'cuts', axis=1, tiled=True)  27.7 us
    all_gather x1, blocking collectives, shards(): right_full = lax.all_gather(right_intersection, 'cuts', axis=1, tiled=True)  25.6 us
  transfers between devices with their start and end apart: 1, of which 1 were waited for; matrix products, arithmetic and copies ran while one was open for 0% of the time, Pallas kernels for 0%

commit v1 on v0

v1 whole, which is shorter than its diff:
```python
import jax
import jax.numpy as jnp
from jax import lax
from jax.experimental import pallas as pl
from jax.experimental.pallas import tpu as pltpu
from jax.sharding import PartitionSpec as P

MESH = pl.DeviceIdType.MESH
SIDE = 4
CHIPS = SIDE * SIDE
OFFSETS = (
    (2, 2),
    (2, 1),
    (2, 3),
    (1, 2),
    (3, 2),
    (1, 1),
    (3, 3),
    (1, 3),
    (3, 1),
    (2, 0),
    (0, 2),
    (1, 0),
    (3, 0),
    (0, 1),
    (0, 3),
)
GROUP = 4


def kernel(
    x_hbm,
    y_hbm,
    l_hbm,
    r_hbm,
    o_ref,
    xv,
    yv,
    lv,
    rv,
    lt,
    tv,
    rc,
    sc,
    part,
    ret,
    local,
    pair_send,
    pair_recv,
    l_send,
    l_recv,
    r_send,
    r_recv,
    t_send,
    t_recv,
    b_send,
    b_recv,
):
    parents, rows = x_hbm.shape[0], x_hbm.shape[1]
    rank = x_hbm.shape[2]
    per_chip = 2 * rows
    me = lax.axis_index("cuts")
    h = me % 2
    chip = me // 2
    x, y = chip // SIDE, chip % SIDE

    def chip_at(dx, dy):
        return ((x + dx) % SIDE) * SIDE + (y + dy) % SIDE

    def remote(src, dst, send, recv, device):
        return pltpu.make_async_remote_copy(
            src_ref=src,
            dst_ref=dst,
            send_sem=send,
            recv_sem=recv,
            device_id={"cuts": device},
            device_id_type=MESH,
        )

    partner = chip * 2 + 1 - h
    ahead = [chip_at(dx, dy) for dx, dy in OFFSETS]
    behind = [chip_at(SIDE - dx, SIDE - dy) for dx, dy in OFFSETS]

    own_l = pltpu.make_async_copy(l_hbm, lv.at[:, chip, h], local.at[0])
    own_r = pltpu.make_async_copy(r_hbm, rv.at[:, chip, h], local.at[1])
    own_x = pltpu.make_async_copy(x_hbm, xv, local.at[2])
    own_y = pltpu.make_async_copy(y_hbm, yv.at[:, h], local.at[3])
    for copy in (own_l, own_r, own_x, own_y):
        copy.start()

    barrier = pltpu.get_barrier_semaphore()
    for c in ahead:
        pl.semaphore_signal(
            barrier, inc=1, device_id={"cuts": 2 * c + h}, device_id_type=MESH
        )
    pl.semaphore_signal(
        barrier, inc=1, device_id={"cuts": partner}, device_id_type=MESH
    )
    pl.semaphore_wait(barrier, CHIPS)

    def spread(ref, send, recv):
        mine = ref.at[:, chip, h]
        return [
            remote(mine, mine, send.at[o], recv.at[o], 2 * c + h)
            for o, c in enumerate(ahead)
        ]

    l_copies = spread(lv, l_send, l_recv)
    r_copies = spread(rv, r_send, r_recv)
    own_l.wait()
    for copy in l_copies:
        copy.start()
    own_r.wait()
    for copy in r_copies:
        copy.start()
    y_pair = remote(y_hbm, yv.at[:, h], pair_send.at[0], pair_recv.at[0], partner)
    y_pair.start()

    def landed(ref, recv, o):
        theirs = ref.at[:, behind[o], h]
        return remote(theirs, theirs, l_send.at[o], recv.at[o], 2 * ahead[o] + h)

    for o in range(CHIPS - 1):
        landed(lv, l_recv, o).wait_recv()
    l_pair = remote(
        lv.at[:, :, h], lv.at[:, :, h], pair_send.at[1], pair_recv.at[1], partner
    )
    l_pair.start()
    own_x.wait()
    l_pair.wait_recv()

    def piece(p, o):
        return remote(
            tv.at[p, ahead[o]],
            rc.at[p, o + 1],
            t_send.at[p, o],
            t_recv.at[p, o],
            2 * ahead[o] + h,
        )

    def give(p, o):
        return remote(
            part.at[p, o + 1],
            ret.at[p, o + 1],
            b_send.at[p, o],
            b_recv.at[p, o],
            2 * behind[o] + h,
        )

    def keep(p):
        return pltpu.make_async_copy(tv.at[p, chip], rc.at[p, 0], local.at[4 + p])

    @pl.loop(0, parents)
    def _(p):
        lt[...] = lv[p].reshape(rank, rank).T

        @pl.loop(0, rows)
        def _(a):
            first = jnp.dot(lt[...], xv[p, a], preferred_element_type=jnp.float32)
            tv[p, :, a] = first.astype(jnp.bfloat16).reshape(CHIPS, per_chip, rank)

        for o in range(CHIPS - 1):
            piece(p, o).start()
        keep(p).start()

    for o in range(CHIPS - 1):
        landed(rv, r_recv, o).wait_recv()
    r_pair = remote(
        rv.at[:, :, h], rv.at[:, :, h], pair_send.at[2], pair_recv.at[2], partner
    )
    r_pair.start()
    own_y.wait()
    y_pair.wait_recv()
    r_pair.wait_recv()

    @pl.loop(0, parents)
    def _(p):
        right = rv[p].reshape(rank, rank)
        for g in range(CHIPS // GROUP):
            if g == 0:
                keep(p).wait()
            slots = range(g * GROUP, (g + 1) * GROUP)
            for s in slots:
                if s:
                    piece(p, s - 1).wait_recv()
            got = rc[p, pl.ds(g * GROUP, GROUP)].reshape(
                GROUP * rows * per_chip, rank
            )
            moved = jnp.dot(got, right, preferred_element_type=jnp.float32)
            sc[0] = moved[:, : rank // 2]
            sc[1] = moved[:, rank // 2 :]
            total = jnp.zeros((GROUP * rows, rank), jnp.float32)
            for k in range(per_chip):
                at = pl.ds(k, GROUP * rows, stride=per_chip)
                second = jnp.concatenate([sc[0, at, :], sc[1, at, :]], axis=1)
                total += jnp.dot(
                    second.astype(jnp.bfloat16),
                    yv[p, k // rows, k % rows],
                    preferred_element_type=jnp.float32,
                )
            part[p, pl.ds(g * GROUP, GROUP)] = total.reshape(GROUP, rows, rank)
            for s in slots:
                if s:
                    give(p, s - 1).start()

    for p in range(parents):
        total = part[p, 0]
        for o in range(CHIPS - 1):
            give(p, o).wait_recv()
            total += ret[p, o + 1]
        o_ref[p] = total

    for copies in (l_copies, r_copies, [y_pair, l_pair, r_pair]):
        for copy in copies:
            copy.wait_send()
    for p in range(parents):
        for o in range(CHIPS - 1):
            piece(p, o).wait_send()
            give(p, o).wait_send()


def shards(core_x, core_y, left, right):
    parents, rows, rank = left.shape
    per_chip = 2 * rows
    bf16, f32 = jnp.bfloat16, jnp.float32
    hops = CHIPS - 1
    dma = pltpu.SemaphoreType.DMA
    return pl.pallas_call(
        kernel,
        out_shape=jax.ShapeDtypeStruct((parents, rows, rank), f32),
        in_specs=[pl.BlockSpec(memory_space=pltpu.HBM)] * 4,
        out_specs=pl.BlockSpec(memory_space=pltpu.VMEM),
        scratch_shapes=[
            pltpu.VMEM((parents, rows, rank, rank), bf16),
            pltpu.VMEM((parents, 2, rows, rank, rank), bf16),
            pltpu.VMEM((parents, CHIPS, 2, rows, rank), bf16),
            pltpu.VMEM((parents, CHIPS, 2, rows, rank), bf16),
            pltpu.VMEM((rank, rank), bf16),
            pltpu.VMEM((parents, CHIPS, rows, per_chip, rank), bf16),
            pltpu.VMEM((parents, CHIPS, rows, per_chip, rank), bf16),
            pltpu.VMEM((2, GROUP * rows * per_chip, rank // 2), f32),
            pltpu.VMEM((parents, CHIPS, rows, rank), f32),
            pltpu.VMEM((parents, CHIPS, rows, rank), f32),
            dma((4 + parents,)),
            dma((3,)),
            dma((3,)),
            dma((hops,)),
            dma((hops,)),
            dma((hops,)),
            dma((hops,)),
            dma((parents, hops)),
            dma((parents, hops)),
            dma((parents, hops)),
            dma((parents, hops)),
        ],
        compiler_params=pltpu.CompilerParams(
            collective_id=0, has_side_effects=True, vmem_limit_bytes=48 << 20
        ),
    )(core_x, core_y, left, right)


def solution(mesh):
    spec4, spec3 = P("node", "cuts", None, None), P("node", "cuts", None)
    return jax.shard_map(
        shards,
        mesh=mesh,
        in_specs=(spec4, spec4, spec3, spec3),
        out_specs=spec3,
        check_vma=False,
    )
```

time: 204 us -> 54.3 us (0.27)
  waiting for transfers between devices: 96.6 us -> 0 us
  blocking collectives: 85.6 us -> 0 us
  Pallas kernels: 0 us -> 48.8 us
  between operations: 13.4 us -> 0.01 us
  matrix products: 4.16 us -> 0 us
  local copies, waits for them, and re-layouts: 2.78 us -> 5.18 us
    reduce_scatter x1 -> x0, waiting for transfers between devices: 96.6 us -> none  [shards(): lax.psum_scatter(jnp.einsum('pakl,pklb->apb', moved, core_y, preferred_el...]
    all_gather x2 -> x0, blocking collectives: 53.2 us -> none  [the longest x1 27.7 us: shards(): left_full = lax.all_gather(left_intersection, 'cuts', axis=1, tiled=True)]
    pallas_call x0 -> x1, Pallas kernels: none -> 48.8 us  [shards(): pl.pallas_call(kernel, out_shape=jax.ShapeDtypeStruct((parents, rows, ran...]
    all_to_all x1 -> x0, blocking collectives: 32.3 us -> none  [shards(): lax.all_to_all(jnp.einsum('pakj,pjl->pakl', first, right_full, preferred_...]
    unnamed x4 -> x9, local copies, waits for them, and re-layouts: 0.01 us -> 5.18 us
    dot_general x2 -> x0, matrix products: 4.16 us -> none  [the longest x1 2.64 us: shards(): jnp.einsum('pakj,pjl->pakl', first, right_full, preferred_element_type=jn...]
    convert_element_type x1 -> x0, local copies, waits for them, and re-layouts: 2.76 us -> none  [shards(): jnp.einsum('pakj,pjl->pakl', first, right_full, preferred_element_type=jn...]
  transfers between devices with their start and end apart: 1 -> 0, of which waited for: 1 -> 0; matrix products, arithmetic and copies ran while one was open for 0% -> 0% of each run, Pallas kernels for 0% -> 0%
where the time goes in v1:
time: 54.3 us; the launch traced here: 54 us
  Pallas kernels  48.8 us (90%)
  local copies, waits for them, and re-layouts  5.18 us (10%)
    pallas_call x1, Pallas kernels, shards(): pl.pallas_call(kernel, out_shape=jax.ShapeDtypeStruct((parents, rows, ran...  48.8 us
    unnamed x9, local copies, waits for them, and re-layouts  5.18 us

profile of v1, /device:TPU:1, one launch (start us, length us, event | category | flops | bytes accessed | tf_op | source)
XLA Modules:
  0.0 54.0 jit_solution(6788878711748088448)
XLA Ops:
  0.0 0.0 copy-start
  0.0 1.6 %copy-done = bf16[2,8,256,256]{3,2,1,0:T(8,128)(2,1)S(1)} copy-done((bf16[2,8,256,256]{3,2,1,0:T(8,128)(2,1)S(1)}, bf16[2,8,256,256]{3,2,1,0:T(8,128)(2,1)}, u32[]{:S(2)}) %copy-start) | copy-done | bytes 2097176
  1.6 0.0 copy-start.1
  1.6 1.6 %copy-done.1 = bf16[2,8,256,256]{3,2,1,0:T(8,128)(2,1)S(1)} copy-done((bf16[2,8,256,256]{3,2,1,0:T(8,128)(2,1)S(1)}, bf16[2,8,256,256]{3,2,1,0:T(8,128)(2,1)}, u32[]{:S(2)}) %copy-start.1) | copy-done | bytes 2097176
  3.2 0.0 copy-start.2
  3.2 0.7 %copy-done.2 = bf16[2,8,256]{2,1,0:T(8,128)(2,1)S(1)} copy-done((bf16[2,8,256]{2,1,0:T(8,128)(2,1)S(1)}, bf16[2,8,256]{2,1,0:T(8,128)(2,1)}, u32[]{:S(2)}) %copy-start.2) | copy-done | bytes 8216
  3.9 0.0 copy-start.3
  3.9 0.7 %copy-done.3 = bf16[2,8,256]{2,1,0:T(8,128)(2,1)S(1)} copy-done((bf16[2,8,256]{2,1,0:T(8,128)(2,1)S(1)}, bf16[2,8,256]{2,1,0:T(8,128)(2,1)}, u32[]{:S(2)}) %copy-start.3) | copy-done | bytes 8216
  4.6 48.8 %shard_map.46 = f32[2,8,256]{2,1,0:T(8,128)S(1)} custom-call(bf16[2,8,256,256]{3,2,1,0:T(8,128)(2,1)S(1)} %copy-done, bf16[2,8,256,256]{3,2,1,0:T(8,128)(2,1)S(1)} %copy-done.1, bf16[2,8,256]{2,1,0:T(8,128)(2,1)S(1)} %copy-done.2, bf16[2,8,256]{2,1,0:T(8,128)(2,1)S(1)} %copy-done.3), custom_call_target="tpu_custom_call" | custom-call | tf_op jit(solution)/shard_map/pallas_call | solution.py:228
  53.4 0.6 %copy.6 = f32[2,8,256]{2,1,0:T(8,128)} copy(f32[2,8,256]{2,1,0:T(8,128)S(1)} %shard_map.46) | data formatting | bytes 32768
Async XLA Ops:
  0.0 1.6 %copy-start = (bf16[2,8,256,256]{3,2,1,0:T(8,128)(2,1)S(1)}, bf16[2,8,256,256]{3,2,1,0:T(8,128)(2,1)}, u32[]{:S(2)}) copy-start(bf16[2,8,256,256]{3,2,1,0:T(8,128)(2,1)} %x_hbm.1) | copy-start | bytes 6291460
  1.6 1.6 %copy-start.1 = (bf16[2,8,256,256]{3,2,1,0:T(8,128)(2,1)S(1)}, bf16[2,8,256,256]{3,2,1,0:T(8,128)(2,1)}, u32[]{:S(2)}) copy-start(bf16[2,8,256,256]{3,2,1,0:T(8,128)(2,1)} %y_hbm.1) | copy-start | bytes 6291460
  3.2 0.7 %copy-start.2 = (bf16[2,8,256]{2,1,0:T(8,128)(2,1)S(1)}, bf16[2,8,256]{2,1,0:T(8,128)(2,1)}, u32[]{:S(2)}) copy-start(bf16[2,8,256]{2,1,0:T(8,128)(2,1)} %l_hbm.1) | copy-start | bytes 24580
  3.9 0.7 %copy-start.3 = (bf16[2,8,256]{2,1,0:T(8,128)(2,1)S(1)}, bf16[2,8,256]{2,1,0:T(8,128)(2,1)}, u32[]{:S(2)}) copy-start(bf16[2,8,256]{2,1,0:T(8,128)(2,1)} %r_hbm.1) | copy-start | bytes 24580

commit v2 on v1

v2 whole, which is shorter than its diff:
```python
import jax
import jax.numpy as jnp
from jax import lax
from jax.experimental import pallas as pl
from jax.experimental.pallas import tpu as pltpu
from jax.sharding import PartitionSpec as P

MESH = pl.DeviceIdType.MESH
SIDE = 4
CHIPS = SIDE * SIDE
OFFSETS = (
    (2, 2),
    (2, 1),
    (2, 3),
    (1, 2),
    (3, 2),
    (1, 1),
    (3, 3),
    (1, 3),
    (3, 1),
    (2, 0),
    (0, 2),
    (1, 0),
    (3, 0),
    (0, 1),
    (0, 3),
)
EVERYONE = tuple((dx, dy, dc) for dx, dy in OFFSETS for dc in (0, 1)) + ((0, 0, 1),)
GROUP = 4


def kernel(
    x_hbm,
    y_hbm,
    l_hbm,
    r_hbm,
    o_ref,
    xv,
    yv,
    lr,
    lt,
    tv,
    rc,
    sc,
    own_part,
    part,
    ret,
    local,
    pair_send,
    pair_recv,
    one_send,
    one_recv,
    rest_send,
    rest_recv,
    hand_send,
    hand_recv,
    t_send,
    t_recv,
    b_send,
    b_recv,
):
    parents, rows = x_hbm.shape[0], x_hbm.shape[1]
    rank = x_hbm.shape[2]
    per_chip = 2 * rows
    me = lax.axis_index("cuts")
    h, chip = lax.rem(me, 2), lax.div(me, 2)
    x, y = lax.div(chip, SIDE), lax.rem(chip, SIDE)
    xs = [SIDE * lax.rem(x + d, SIDE) for d in range(SIDE)]
    ys = [lax.rem(y + d, SIDE) for d in range(SIDE)]

    def chip_at(dx, dy):
        return xs[dx % SIDE] + ys[dy % SIDE]

    def remote(src, dst, send, recv, device):
        return pltpu.make_async_remote_copy(
            src_ref=src,
            dst_ref=dst,
            send_sem=send,
            recv_sem=recv,
            device_id={"cuts": device},
            device_id_type=MESH,
        )

    partner = chip * 2 + 1 - h
    ahead = [chip_at(dx, dy) for dx, dy in OFFSETS]
    behind = [chip_at(SIDE - dx, SIDE - dy) for dx, dy in OFFSETS]

    own_l = pltpu.make_async_copy(l_hbm, lr.at[pl.ds(0, parents), chip, h], local.at[0])
    own_r = pltpu.make_async_copy(r_hbm, lr.at[pl.ds(parents, parents), chip, h], local.at[1])
    own_x = pltpu.make_async_copy(x_hbm, xv, local.at[2])
    own_y = pltpu.make_async_copy(y_hbm, yv.at[:, h], local.at[3])
    for copy in (own_l, own_r, own_x, own_y):
        copy.start()

    first_plane = lax.axis_index("node") == 0
    absent = jnp.where(first_plane, 0, -1)
    late = jnp.logical_and(first_plane, me == 0)
    helper = jnp.logical_and(first_plane, me == 1)
    others = [
        (2 * chip_at(dx, dy) + (1 - h if dc else h), dc) for dx, dy, dc in EVERYONE
    ]
    barrier = pltpu.get_barrier_semaphore()

    @pl.when(jnp.logical_not(late))
    def _():
        for to, _ in others:
            pl.semaphore_signal(
                barrier, inc=1, device_id={"cuts": to}, device_id_type=MESH
            )

    met = jnp.logical_or(late, jnp.logical_not(first_plane))
    pl.semaphore_wait(barrier, jnp.where(met, len(others), len(others) - 1))

    later = pl.ds(1, 2 * parents - 1)

    def one(o):
        to, dc = others[o]
        mine = lr.at[0, chip, h]
        return remote(mine, mine, one_send.at[dc], one_recv.at[dc], to)

    def ones(count, dc):
        blocks = lr.at[0, pl.ds(CHIPS - count, count), 0]
        return remote(blocks, blocks, one_send.at[dc], one_recv.at[dc], partner)

    def rest(o):
        mine = lr.at[later, chip, h]
        return remote(
            mine, mine, rest_send.at[0], rest_recv.at[0], 2 * ahead[o] + h
        )

    def rests():
        blocks = lr.at[later, pl.ds(1, CHIPS - 1), 0]
        return remote(blocks, blocks, rest_send.at[0], rest_recv.at[0], partner)

    def rest_pair():
        rows_of = lr.at[later, :, h]
        return remote(rows_of, rows_of, pair_send.at[0], pair_recv.at[0], partner)

    def hand():
        own, most = lr.at[0, 0, 1], lr.at[0, pl.ds(1, CHIPS - 1)]
        return (
            remote(own, own, hand_send.at[0], hand_recv.at[0], 0),
            remote(most, most, hand_send.at[1], hand_recv.at[1], 0),
        )

    y_pair = [
        remote(
            y_hbm.at[p],
            yv.at[p, h],
            pair_send.at[1 + p],
            pair_recv.at[1 + p],
            partner,
        )
        for p in range(parents)
    ]

    own_l.wait()
    for o in range(len(others)):

        @pl.when(others[o][0] != absent)
        def _():
            one(o).start()

    own_r.wait()
    for o in range(CHIPS - 1):

        @pl.when(2 * ahead[o] + h != absent)
        def _():
            rest(o).start()

    @pl.when(partner != absent)
    def _():
        for copy in y_pair:
            copy.start()

    @pl.when(jnp.logical_not(late))
    def _():
        ones(CHIPS - 1, 0).wait_recv()
        ones(CHIPS, 1).wait_recv()

    @pl.when(helper)
    def _():
        for copy in hand() + tuple(y_pair):
            copy.start()

    @pl.when(late)
    def _():
        for copy in hand():
            copy.wait_recv()

    for o in range(CHIPS - 1):

        @pl.when(2 * ahead[o] + h == absent)
        def _():
            rest(o).start()

    def piece(p, o):
        return remote(
            tv.at[p, ahead[o]],
            rc.at[p, o + 1],
            t_send.at[p],
            t_recv.at[p, (o + 1) // GROUP],
            2 * ahead[o] + h,
        )

    def pieces(p, g):
        slots = pl.ds(max(g * GROUP, 1), GROUP - (g == 0))
        return remote(
            rc.at[p, slots], rc.at[p, slots], t_send.at[p], t_recv.at[p, g], partner
        )

    def give(p, o):
        return remote(
            part.at[p, o + 1],
            ret.at[p, o + 1],
            b_send.at[p],
            b_recv.at[p],
            2 * behind[o] + h,
        )

    def all_of(ref, send, recv, p):
        blocks = ref.at[p, pl.ds(1, CHIPS - 1)]
        return remote(blocks, blocks, send.at[p], recv.at[p], partner)

    def keep(p):
        return pltpu.make_async_copy(tv.at[p, chip], rc.at[p, 0], local.at[4 + p])

    own_x.wait()
    for p in range(parents):
        lt[...] = lr[p].reshape(rank, rank).T

        @pl.loop(0, rows)
        def _(a):
            first = jnp.dot(lt[...], xv[p, a], preferred_element_type=jnp.float32)
            tv[p, :, a] = first.astype(jnp.bfloat16).reshape(CHIPS, per_chip, rank)

        for o in range(CHIPS - 1):
            piece(p, o).start()
        keep(p).start()
        if p == 0:
            rests().wait_recv()
            rest_pair().start()
            rest_pair().wait_recv()

    own_y.wait()
    for copy in y_pair:
        copy.wait_recv()

    skips = [jnp.logical_and(first_plane, jnp.logical_and(h == dc, me != 0)) for dc in (0, 1)]
    for dc in (0, 1):

        @pl.when(skips[dc])
        def _():
            ones(CHIPS - 2 + dc, dc).wait_send()

        @pl.when(jnp.logical_not(skips[dc]))
        def _():
            ones(CHIPS - 1 + dc, dc).wait_send()

    rests().wait_send()
    rest_pair().wait_send()
    for copy in y_pair:
        copy.wait_send()

    @pl.when(helper)
    def _():
        for copy in hand():
            copy.wait_send()

    @pl.loop(0, parents)
    def _(p):
        weights = lr[parents + p].reshape(rank, rank)
        for g in range(CHIPS // GROUP):
            if g == 0:
                keep(p).wait()
            slots = range(g * GROUP, (g + 1) * GROUP)
            pieces(p, g).wait_recv()
            got = rc[p, pl.ds(g * GROUP, GROUP)].reshape(
                GROUP * rows * per_chip, rank
            )
            moved = jnp.dot(got, weights, preferred_element_type=jnp.float32)
            sc[0] = moved[:, : rank // 2]
            sc[1] = moved[:, rank // 2 :]
            total = jnp.zeros((GROUP * rows, rank), jnp.float32)
            for k in range(per_chip):
                at = pl.ds(k, GROUP * rows, stride=per_chip)
                second = jnp.concatenate([sc[0, at, :], sc[1, at, :]], axis=1)
                total += jnp.dot(
                    second.astype(jnp.bfloat16),
                    yv[p, k // rows, k % rows],
                    preferred_element_type=jnp.float32,
                )
            whole = total.reshape(GROUP, rows, rank)
            if g == 0:
                own_part[p] = whole[0]
            part[p, pl.ds(g * GROUP, GROUP)] = whole.astype(jnp.bfloat16)
            for s in slots:
                if s:
                    give(p, s - 1).start()

    for p in range(parents):
        all_of(ret, b_send, b_recv, p).wait_recv()
        returned = ret[p, pl.ds(1, CHIPS - 1)].astype(jnp.float32)
        o_ref[p] = own_part[p] + jnp.sum(returned, axis=0)

    for p in range(parents):
        all_of(tv, t_send, b_recv, p).wait_send()
        all_of(part, b_send, b_recv, p).wait_send()


def shards(*arrays):
    parents, rows, rank = arrays[2].shape
    per_chip = 2 * rows
    bf16, f32 = jnp.bfloat16, jnp.float32
    dma = pltpu.SemaphoreType.DMA
    return pl.pallas_call(
        kernel,
        out_shape=jax.ShapeDtypeStruct((parents, rows, rank), f32),
        in_specs=[pl.BlockSpec(memory_space=pltpu.HBM)] * 4,
        out_specs=pl.BlockSpec(memory_space=pltpu.VMEM),
        scratch_shapes=[
            pltpu.VMEM((parents, rows, rank, rank), bf16),
            pltpu.VMEM((parents, 2, rows, rank, rank), bf16),
            pltpu.VMEM((2 * parents, CHIPS, 2, rows, rank), bf16),
            pltpu.VMEM((rank, rank), bf16),
            pltpu.VMEM((parents, CHIPS, rows, per_chip, rank), bf16),
            pltpu.VMEM((parents, CHIPS, rows, per_chip, rank), bf16),
            pltpu.VMEM((2, GROUP * rows * per_chip, rank // 2), f32),
            pltpu.VMEM((parents, rows, rank), f32),
            pltpu.VMEM((parents, CHIPS, rows, rank), bf16),
            pltpu.VMEM((parents, CHIPS, rows, rank), bf16),
            dma((4 + parents,)),
            dma((1 + parents,)),
            dma((1 + parents,)),
            dma((2,)),
            dma((2,)),
            dma((1,)),
            dma((1,)),
            dma((2,)),
            dma((2,)),
            dma((parents,)),
            dma((parents, CHIPS // GROUP)),
            dma((parents,)),
            dma((parents,)),
        ],
        compiler_params=pltpu.CompilerParams(
            collective_id=0, has_side_effects=True, vmem_limit_bytes=48 << 20
        ),
    )(*(pltpu.with_memory_space_constraint(v, pltpu.HBM) for v in arrays))


def solution(mesh):
    spec4, spec3 = P("node", "cuts", None, None), P("node", "cuts", None)
    return jax.shard_map(
        shards,
        mesh=mesh,
        in_specs=(spec4, spec4, spec3, spec3),
        out_specs=spec3,
        check_vma=False,
    )
```

time: 54.3 us -> 46.7 us (0.86)
  the two profiles are of different devices: /device:TPU:1 before, /device:TPU:224 now
where the time goes in v2:
time: 46.7 us; the launch traced here: 46.6 us
  Pallas kernels  46 us (99%)
  local copies, waits for them, and re-layouts  0.61 us (1%)
    pallas_call x1, Pallas kernels, shards(): pl.pallas_call(kernel, out_shape=jax.ShapeDtypeStruct((parents, rows, ran...  46 us

profile of v2, /device:TPU:224, one launch (start us, length us, event | category | flops | bytes accessed | tf_op | source)
XLA Modules:
  0.0 46.6 jit_solution(12161412864720737644)
XLA Ops:
  0.0 46.0 %shard_map.46 = f32[2,8,256]{2,1,0:T(8,128)S(1)} custom-call(bf16[2,8,256,256]{3,2,1,0:T(8,128)(2,1)} %x_hbm.1, bf16[2,8,256,256]{3,2,1,0:T(8,128)(2,1)} %y_hbm.1, bf16[2,8,256]{2,1,0:T(8,128)(2,1)} %l_hbm.1, bf16[2,8,256]{2,1,0:T(8,128)(2,1)} %r_hbm.1), custom_call_target="tpu_custom_call" | custom-call | tf_op jit(solution)/shard_map/pallas_call | solution.py:316
  46.0 0.6 %copy.6 = f32[2,8,256]{2,1,0:T(8,128)} copy(f32[2,8,256]{2,1,0:T(8,128)S(1)} %shard_map.46) | data formatting | bytes 32768

commit v3 on v2

--- a/solution.py
+++ b/solution.py
@@ -194,10 +194,13 @@
         def _():
             rest(o).start()
 
-    def piece(p, o):
+    half = rows // 2
+
+    def piece(p, o, part_of):
+        some = pl.ds(part_of * half, half)
         return remote(
-            tv.at[p, ahead[o]],
-            rc.at[p, o + 1],
+            tv.at[p, ahead[o], some],
+            rc.at[p, o + 1, some],
             t_send.at[p],
             t_recv.at[p, (o + 1) // GROUP],
             2 * ahead[o] + h,
@@ -229,13 +232,13 @@
     for p in range(parents):
         lt[...] = lr[p].reshape(rank, rank).T
 
-        @pl.loop(0, rows)
-        def _(a):
-            first = jnp.dot(lt[...], xv[p, a], preferred_element_type=jnp.float32)
-            tv[p, :, a] = first.astype(jnp.bfloat16).reshape(CHIPS, per_chip, rank)
-
-        for o in range(CHIPS - 1):
-            piece(p, o).start()
+        for part_of in range(2):
+            for a in range(part_of * half, (part_of + 1) * half):
+                first = jnp.dot(lt[...], xv[p, a], preferred_element_type=jnp.float32)
+                tv[p, :, a] = first.astype(jnp.bfloat16).reshape(CHIPS, per_chip, rank)
+            for o in range(CHIPS - 1):
+                piece(p, o, part_of).start()
+
         keep(p).start()
         if p == 0:
             rests().wait_recv()

time: 46.7 us -> 43.2 us (0.925)
  the two profiles are of different devices: /device:TPU:224 before, /device:TPU:1 now
where the time goes in v3:
time: 43.2 us; the launch traced here: 43.1 us
  Pallas kernels  42.5 us (98%)
  local copies, waits for them, and re-layouts  0.61 us (1%)
    pallas_call x1, Pallas kernels, shards(): pl.pallas_call(kernel, out_shape=jax.ShapeDtypeStruct((parents, rows, ran...  42.5 us

profile of v3, /device:TPU:1, one launch (start us, length us, event | category | flops | bytes accessed | tf_op | source)
XLA Modules:
  0.0 43.1 jit_solution(1271424512843859448)
XLA Ops:
  0.0 42.5 %shard_map.46 = f32[2,8,256]{2,1,0:T(8,128)S(1)} custom-call(bf16[2,8,256,256]{3,2,1,0:T(8,128)(2,1)} %x_hbm.1, bf16[2,8,256,256]{3,2,1,0:T(8,128)(2,1)} %y_hbm.1, bf16[2,8,256]{2,1,0:T(8,128)(2,1)} %l_hbm.1, bf16[2,8,256]{2,1,0:T(8,128)(2,1)} %r_hbm.1), custom_call_target="tpu_custom_call" | custom-call | tf_op jit(solution)/shard_map/pallas_call | solution.py:319
  42.5 0.6 %copy.6 = f32[2,8,256]{2,1,0:T(8,128)} copy(f32[2,8,256]{2,1,0:T(8,128)S(1)} %shard_map.46) | data formatting | bytes 32768

commit v4 on v3

--- a/solution.py
+++ b/solution.py
@@ -25,8 +25,10 @@
     (0, 1),
     (0, 3),
 )
-EVERYONE = tuple((dx, dy, dc) for dx, dy in OFFSETS for dc in (0, 1)) + ((0, 0, 1),)
+EVERYONE = ((0, 0, 1),) + tuple((dx, dy, dc) for dx, dy in OFFSETS for dc in (0, 1))
 GROUP = 4
+HELD = 4
+HOLD_AFTER = 3
 
 
 def kernel(
@@ -85,29 +87,30 @@
     ahead = [chip_at(dx, dy) for dx, dy in OFFSETS]
     behind = [chip_at(SIDE - dx, SIDE - dy) for dx, dy in OFFSETS]
 
-    own_l = pltpu.make_async_copy(l_hbm, lr.at[pl.ds(0, parents), chip, h], local.at[0])
-    own_r = pltpu.make_async_copy(r_hbm, lr.at[pl.ds(parents, parents), chip, h], local.at[1])
+    first_plane = lax.axis_index("node") == 0
+    absent = jnp.where(first_plane, 0, -1)
+    late = jnp.logical_and(first_plane, me == 0)
+    helper = jnp.logical_and(first_plane, me == 1)
+    hold = jnp.logical_not(first_plane)
+    others = [
+        (2 * chip_at(dx, dy) + (1 - h if dc else h), dc) for dx, dy, dc in EVERYONE
+    ]
+    barrier = pltpu.get_barrier_semaphore()
+
+    @pl.when(jnp.logical_not(late))
+    def _():
+        for to, _ in others:
+            pl.semaphore_signal(
+                barrier, inc=1, device_id={"cuts": to}, device_id_type=MESH
+            )
+
+    own_l = pltpu.make_async_copy(l_hbm, lr.at[pl.ds(0, parents), h, chip], local.at[0])
+    own_r = pltpu.make_async_copy(r_hbm, lr.at[pl.ds(parents, parents), h, chip], local.at[1])
     own_x = pltpu.make_async_copy(x_hbm, xv, local.at[2])
     own_y = pltpu.make_async_copy(y_hbm, yv.at[:, h], local.at[3])
     for copy in (own_l, own_r, own_x, own_y):
         copy.start()
 
-    first_plane = lax.axis_index("node") == 0
-    absent = jnp.where(first_plane, 0, -1)
-    late = jnp.logical_and(first_plane, me == 0)
-    helper = jnp.logical_and(first_plane, me == 1)
-    others = [
-        (2 * chip_at(dx, dy) + (1 - h if dc else h), dc) for dx, dy, dc in EVERYONE
-    ]
-    barrier = pltpu.get_barrier_semaphore()
-
-    @pl.when(jnp.logical_not(late))
-    def _():
-        for to, _ in others:
-            pl.semaphore_signal(
-                barrier, inc=1, device_id={"cuts": to}, device_id_type=MESH
-            )
-
     met = jnp.logical_or(late, jnp.logical_not(first_plane))
     pl.semaphore_wait(barrier, jnp.where(met, len(others), len(others) - 1))
 
@@ -115,29 +118,32 @@
 
     def one(o):
         to, dc = others[o]
-        mine = lr.at[0, chip, h]
+        mine = lr.at[0, h, chip]
         return remote(mine, mine, one_send.at[dc], one_recv.at[dc], to)
 
+    def matrix(i):
+        return jnp.swapaxes(lr[i], 0, 1).reshape(rank, rank)
+
     def ones(count, dc):
-        blocks = lr.at[0, pl.ds(CHIPS - count, count), 0]
+        blocks = lr.at[0, 0, pl.ds(CHIPS - count, count)]
         return remote(blocks, blocks, one_send.at[dc], one_recv.at[dc], partner)
 
     def rest(o):
-        mine = lr.at[later, chip, h]
+        mine = lr.at[later, h, chip]
         return remote(
             mine, mine, rest_send.at[0], rest_recv.at[0], 2 * ahead[o] + h
         )
 
     def rests():
-        blocks = lr.at[later, pl.ds(1, CHIPS - 1), 0]
+        blocks = lr.at[later, 0, pl.ds(1, CHIPS - 1)]
         return remote(blocks, blocks, rest_send.at[0], rest_recv.at[0], partner)
 
     def rest_pair():
-        rows_of = lr.at[later, :, h]
+        rows_of = lr.at[later, h]
         return remote(rows_of, rows_of, pair_send.at[0], pair_recv.at[0], partner)
 
     def hand():
-        own, most = lr.at[0, 0, 1], lr.at[0, pl.ds(1, CHIPS - 1)]
+        own, most = lr.at[0, 1, 0], lr.at[0, :, pl.ds(1, CHIPS - 1)]
         return (
             remote(own, own, hand_send.at[0], hand_recv.at[0], 0),
             remote(most, most, hand_send.at[1], hand_recv.at[1], 0),
@@ -230,19 +236,26 @@
 
     own_x.wait()
     for p in range(parents):
-        lt[...] = lr[p].reshape(rank, rank).T
+        lt[...] = matrix(p).T
 
         for part_of in range(2):
             for a in range(part_of * half, (part_of + 1) * half):
                 first = jnp.dot(lt[...], xv[p, a], preferred_element_type=jnp.float32)
                 tv[p, :, a] = first.astype(jnp.bfloat16).reshape(CHIPS, per_chip, rank)
-            for o in range(CHIPS - 1):
+            if p == 0 and part_of == 1:
+                rests().wait_recv()
+                rest_pair().start()
+            for o in range(CHIPS - 1 if p == 0 else CHIPS - 1 - HELD):
                 piece(p, o, part_of).start()
+            if p == parents - 1:
+
+                @pl.when(jnp.logical_not(hold))
+                def _():
+                    for o in range(CHIPS - 1 - HELD, CHIPS - 1):
+                        piece(p, o, part_of).start()
 
         keep(p).start()
         if p == 0:
-            rests().wait_recv()
-            rest_pair().start()
             rest_pair().wait_recv()
 
     own_y.wait()
@@ -272,7 +285,7 @@
 
     @pl.loop(0, parents)
     def _(p):
-        weights = lr[parents + p].reshape(rank, rank)
+        weights = matrix(parents + p)
         for g in range(CHIPS // GROUP):
             if g == 0:
                 keep(p).wait()
@@ -300,6 +313,14 @@
             for s in slots:
                 if s:
                     give(p, s - 1).start()
+            if g == HOLD_AFTER:
+
+                @pl.when(jnp.logical_and(p == 0, hold))
+                def _():
+                    for o in range(CHIPS - 1 - HELD, CHIPS - 1):
+                        for part_of in range(2):
+                            piece(parents - 1, o, part_of).start()
+
 
     for p in range(parents):
         all_of(ret, b_send, b_recv, p).wait_recv()
@@ -324,7 +345,7 @@
         scratch_shapes=[
             pltpu.VMEM((parents, rows, rank, rank), bf16),
             pltpu.VMEM((parents, 2, rows, rank, rank), bf16),
-            pltpu.VMEM((2 * parents, CHIPS, 2, rows, rank), bf16),
+            pltpu.VMEM((2 * parents, 2, CHIPS, rows, rank), bf16),
             pltpu.VMEM((rank, rank), bf16),
             pltpu.VMEM((parents, CHIPS, rows, per_chip, rank), bf16),
             pltpu.VMEM((parents, CHIPS, rows, per_chip, rank), bf16),

time: 43.2 us -> 43.3 us (level)
  no operation moved by 1% of the time
where the time goes in v4:
time: 43.3 us; the launch traced here: 43.1 us
  Pallas kernels  42.5 us (98%)
  local copies, waits for them, and re-layouts  0.61 us (1%)
    pallas_call x1, Pallas kernels, shards(): pl.pallas_call(kernel, out_shape=jax.ShapeDtypeStruct((parents, rows, ran...  42.5 us

profile of v4, /device:TPU:1, one launch (start us, length us, event | category | flops | bytes accessed | tf_op | source)
XLA Modules:
  0.0 43.1 jit_solution(18070057952318653235)
XLA Ops:
  0.0 42.5 %shard_map.46 = f32[2,8,256]{2,1,0:T(8,128)S(1)} custom-call(bf16[2,8,256,256]{3,2,1,0:T(8,128)(2,1)} %x_hbm.1, bf16[2,8,256,256]{3,2,1,0:T(8,128)(2,1)} %y_hbm.1, bf16[2,8,256]{2,1,0:T(8,128)(2,1)} %l_hbm.1, bf16[2,8,256]{2,1,0:T(8,128)(2,1)} %r_hbm.1), custom_call_target="tpu_custom_call" | custom-call | tf_op jit(solution)/shard_map/pallas_call | solution.py:340
  42.5 0.6 %copy.6 = f32[2,8,256]{2,1,0:T(8,128)} copy(f32[2,8,256]{2,1,0:T(8,128)S(1)} %shard_map.46) | data formatting | bytes 32768
